TPU v7x, 128 devices: a whole 4x4x4 slice. The times are simulated.
128 devices in a mesh: section: 2 (over core), dp: 64 (over y, z, x).
Axes of the slice: x: 4, y: 4, z: 4, core: 2. Of those that a mesh axis runs over, the one named last changes fastest.
Arguments:
- inputs: bfloat16 [2, 4096, 960], P(None, 'dp'), may hold values from -16 to 16
- starts: int32 [2, 4096], P(None, 'dp'), may hold values from 0 to 64, as said below
- cotangent: bfloat16 [2, 4096, 960], P(None, 'dp'), may hold values from -16 to 16
- w_query: bfloat16 [2, 960, 960], P('section', 'dp'), may hold values from -0.1875 to 0.1875
- w_key: bfloat16 [2, 960, 320], P('section', 'dp'), may hold values from -0.1875 to 0.1875
- w_value: bfloat16 [2, 960, 320], P('section', 'dp'), may hold values from -0.1875 to 0.1875
- w_output: bfloat16 [2, 960, 960], P('section', 'dp'), may hold values from -0.75 to 0.75
- w_gate: bfloat16 [2, 960, 2560], P('section', 'dp'), may hold values from -0.1875 to 0.1875
- w_up: bfloat16 [2, 960, 2560], P('section', 'dp'), may hold values from -0.1875 to 0.1875
- w_down: bfloat16 [2, 2560, 960], P('section', 'dp'), may hold values from -0.15625 to 0.15625
- attn_gain: bfloat16 [2, 960], P('section', 'dp'), may hold values from 0.25 to 1.75
- ffn_gain: bfloat16 [2, 960], P('section', 'dp'), may hold values from 0.25 to 1.75
Outputs:
- activations: bfloat16 [2, 2, 4096, 960], P('section', None, 'dp')
- input_grads: bfloat16 [2, 2, 4096, 960], P('section', None, 'dp')
- grad_query: float32 [2, 960, 960], P('section', 'dp')
- grad_key: float32 [2, 960, 320], P('section', 'dp')
- grad_value: float32 [2, 960, 320], P('section', 'dp')
- grad_output: float32 [2, 960, 960], P('section', 'dp')
- grad_gate: float32 [2, 960, 2560], P('section', 'dp')
- grad_up: float32 [2, 960, 2560], P('section', 'dp')
- grad_down: float32 [2, 2560, 960], P('section', 'dp')
- grad_attn_gain: float32 [2, 960], P('section', 'dp')
- grad_ffn_gain: float32 [2, 960], P('section', 'dp')
Inputs may be any that keep to these rules, and one draw needn't show every extreme that they name: `starts`: within each aligned block of 64 rows (one index of dp, one micro-batch) sequences lie end to end from the block's first row, each row holding the block-local index of its sequence's first row; the rows after the last sequence are padding and hold 64. At least a quarter of every block's rows are in sequences, and some blocks are full.
All inputs are finite; a program needn't handle non-finite values.
Results may differ from a plain program's by a relative error of at most 0.023.
Values may be sent and summed in bfloat16 or wider, within the bound.
No kernel may reach another device: no remote copies, remote signals or barrier semaphores. Data moves between devices by JAX's collectives and lax.ppermute only.
A program may use at most 256 MiB of HBM per device.

v0:
```python
import jax
import jax.numpy as jnp
from jax import lax
from jax.sharding import PartitionSpec as P

D = 960
HEADS = 15
KV_HEADS = 5
GROUP = HEADS // KV_HEADS
HEAD_DIM = 64
FF = 2560
QD = 960
KVD = 320
OWNERS = 64
SLOT = 15
PADDED = 16
DOWN_ROWS = 40
norm_eps = 1e-05
masked_score = -1e30
rope_base = 10000.0
f32 = jnp.float32
bf16 = jnp.bfloat16


def gray(value):
    return value ^ value >> 1


AXIS_SHIFT = {"y": 4, "z": 2, "x": 0}
BITS = (("y", 1), ("y", 0), ("z", 1), ("z", 0), ("x", 1), ("x", 0))


def partner_pairs(bit):
    axis, place = bit
    shift = AXIS_SHIFT[axis]
    pairs = []
    for source in range(OWNERS):
        coordinate = source >> shift & 3
        other = gray(gray(coordinate) ^ 1 << place)
        pairs.append((source, source + (other - coordinate << shift)))
    return pairs


def owner_of(position):
    me = lax.axis_index("dp")
    owner = 0
    for shift in (4, 2, 0):
        owner = owner + (gray(gray(me >> shift & 3) ^ position >> shift & 3) << shift)
    return owner


def dot(left, right):
    return jnp.dot(left, right, preferred_element_type=f32)


def dot_t(left, right):
    return lax.dot_general(left, right, (((1,), (1,)), ((), ())), preferred_element_type=f32)


def spread_matrix():
    row = lax.broadcasted_iota(jnp.int32, (D, OWNERS * PADDED), 0)
    col = lax.broadcasted_iota(jnp.int32, (D, OWNERS * PADDED), 1)
    return ((row == SLOT * (col // PADDED) + col % PADDED) & (col % PADDED < SLOT)).astype(bf16)


def own_spread():
    row = lax.broadcasted_iota(jnp.int32, (OWNERS * PADDED, D), 0)
    col = lax.broadcasted_iota(jnp.int32, (OWNERS * PADDED, D), 1)
    owner = owner_of(row // PADDED)
    return ((col == SLOT * owner + row % PADDED) & (row % PADDED < SLOT)).astype(bf16)


def gather_rows(values, spread):
    high = values.astype(bf16)
    low = (values - high.astype(f32)).astype(bf16)
    return dot_t(high, spread) + dot_t(low, spread)


def geometry(starts):
    rows = starts.shape[-1]
    local = jnp.arange(rows, dtype=jnp.int32)
    live = starts <= local
    position = jnp.where(live, local - starts, 0).astype(f32)
    frequency = rope_base ** (-2.0 * jnp.arange(HEAD_DIM // 2, dtype=f32) / HEAD_DIM)
    angles = position[..., None, None] * frequency
    causal = local[None, :] <= local[:, None]
    inside = local >= starts[..., None]
    diagonal = local[None, :] == local[:, None]
    allowed = causal & inside | diagonal
    return (live.astype(f32).reshape(-1, 1), jnp.cos(angles), jnp.sin(angles), allowed)


def rotate(values, cosine, sine):
    half = HEAD_DIM // 2
    first, second = (values[..., :half], values[..., half:])
    return jnp.concatenate(
        [first * cosine - second * sine, second * cosine + first * sine], axis=-1
    )


def norm_parts(values):
    inverse = lax.rsqrt(jnp.mean(values * values, axis=-1, keepdims=True) + norm_eps)
    return (values * inverse, inverse)


def norm_back(grad, normal, inverse, gain):
    scaled = grad * gain
    return inverse * (scaled - normal * jnp.mean(scaled * normal, axis=-1, keepdims=True))


def forward(source, weights, geo, spread):
    w_query, w_key, w_value, w_output, w_gate, w_up, w_down, attn_gain, ffn_gain = weights
    live, cosine, sine, allowed = geo
    micro, rows = cosine.shape[:2]
    h = source.astype(f32)
    n1, r1 = norm_parts(h)
    a = (n1 * attn_gain).astype(bf16)
    a_wide = dot(a, spread).astype(bf16)
    q = rotate(dot(a_wide, w_query).reshape(micro, rows, HEADS, HEAD_DIM), cosine, sine)
    k = rotate(dot(a_wide, w_key).reshape(micro, rows, KV_HEADS, HEAD_DIM), cosine, sine)
    v = dot(a_wide, w_value).astype(bf16).reshape(micro, rows, KV_HEADS, HEAD_DIM)
    q = q.astype(bf16).reshape(micro, rows, KV_HEADS, GROUP, HEAD_DIM)
    k = k.astype(bf16)
    s = jnp.einsum("bqhgd,bkhd->bhgqk", q, k, preferred_element_type=f32) * HEAD_DIM ** (-0.5)
    s = jnp.where(allowed[:, None, None], s, masked_score)
    e = jnp.exp(s - jnp.max(s, axis=-1, keepdims=True))
    p = e / jnp.sum(e, axis=-1, keepdims=True)
    p_low = p.astype(bf16)
    o = jnp.einsum("bhgqk,bkhd->bqhgd", p_low, v, preferred_element_type=f32)
    o = o.reshape(micro * rows, QD).astype(bf16)
    m = h + dot(dot(o, spread).astype(bf16), w_output)
    n2, r2 = norm_parts(m)
    b = (n2 * ffn_gain).astype(bf16)
    b_wide = dot(b, spread).astype(bf16)
    gate = dot(b_wide, w_gate)
    up = dot(b_wide, w_up)
    hidden = (gate * jax.nn.sigmoid(gate) * up).astype(bf16)
    result = ((m + dot(hidden, w_down)) * live).astype(bf16)
    return (result, (n1, r1, a, q, k, v, p, p_low, o, n2, r2, b, gate, up, hidden))


def backward(saved, upstream, weights, geo, spread):
    w_query, w_key, w_value, w_output, w_gate, w_up, w_down, attn_gain, ffn_gain = weights
    n1, r1, a, q, k, v, p, p_low, o, n2, r2, b, gate, up, hidden = saved
    live, cosine, sine, allowed = geo
    micro, rows = cosine.shape[:2]
    d3 = upstream.astype(f32) * live
    d3_low = d3.astype(bf16)
    dhidden = dot_t(d3_low, w_down)
    sig = jax.nn.sigmoid(gate)
    dg = (dhidden * up * sig * (1.0 + gate * (1.0 - sig))).astype(bf16)
    du = (dhidden * gate * sig).astype(bf16)
    db = gather_rows(dot_t(dg, w_gate) + dot_t(du, w_up), spread)
    dm = d3 + norm_back(db, n2, r2, ffn_gain)
    dffn = jnp.sum(db * n2, axis=0)
    dm_low = dm.astype(bf16)
    do = dot_t(dot_t(dm_low, w_output).astype(bf16), spread).astype(bf16)
    do = do.reshape(micro, rows, KV_HEADS, GROUP, HEAD_DIM)
    dp = jnp.einsum("bqhgd,bkhd->bhgqk", do, v, preferred_element_type=f32)
    dv = jnp.einsum("bhgqk,bqhgd->bkhd", p_low, do, preferred_element_type=f32)
    ds = (p * (dp - jnp.sum(p * dp, axis=-1, keepdims=True))).astype(bf16)
    dq = jnp.einsum("bhgqk,bkhd->bqhgd", ds, k, preferred_element_type=f32) * HEAD_DIM ** (-0.5)
    dk = jnp.einsum("bhgqk,bqhgd->bkhd", ds, q, preferred_element_type=f32) * HEAD_DIM ** (-0.5)
    dq = rotate(dq.reshape(micro, rows, HEADS, HEAD_DIM), cosine, -sine)
    dq = dq.reshape(micro * rows, QD).astype(bf16)
    dk = rotate(dk, cosine, -sine).reshape(micro * rows, KVD).astype(bf16)
    dv = dv.reshape(micro * rows, KVD).astype(bf16)
    da = gather_rows(dot_t(dq, w_query) + dot_t(dk, w_key) + dot_t(dv, w_value), spread)
    dh = dm + norm_back(da, n1, r1, attn_gain)
    dattn = jnp.sum(da * n1, axis=0)
    return (dh.astype(bf16), (d3_low, dg, du, dm_low, dq, dk, dv, dattn, dffn))


def blocks(left_t, rows):
    return left_t.reshape((2,) * 6 + (rows, left_t.shape[-1]))


def pick(array, dim, index):
    return lax.index_in_dim(array, index, dim, keepdims=False)


def product(left_t, right):
    flat = left_t.reshape(-1, left_t.shape[-1])
    return dot(flat, right).reshape(left_t.shape[:-1] + (right.shape[-1],))


def first_halves(left_t, right, order, extra=None):
    dim = BITS.index(order[0])
    halves = []
    for index in (1, 0):
        value = product(pick(left_t, dim, index), right)
        if extra is not None:
            value = value + pick(extra, dim, index)
        halves.append(value.astype(bf16))
    return (halves[1], halves[0])


def rotations(place, then):
    axes = "yzx"
    result = []
    for turn in range(3):
        turned = axes[turn:] + axes[:turn]
        result.append(
            tuple(((axis, place) for axis in turned)) + tuple(((axis, then) for axis in turned))
        )
    return result


ORDERS = (rotations(1, 0), rotations(0, 1))


def halving(kept, sent, order, left, last):
    bit = order[0]
    left = [other for other in left if other != bit]
    arrived = lax.ppermute(sent, "dp", partner_pairs(bit))
    if len(order) == 1:
        return (kept.astype(f32) + arrived.astype(f32), None, left)
    if last:
        return ((kept.astype(f32) + arrived.astype(f32)).astype(bf16), None, left)
    dim = left.index(order[1])
    next_sent = pick(kept, dim, 1).astype(f32) + pick(arrived, dim, 1).astype(f32)
    next_kept = pick(kept, dim, 0).astype(f32) + pick(arrived, dim, 0).astype(f32)
    return (next_kept.astype(bf16), next_sent.astype(bf16), left)


def reduce_three(members, orders):
    after = []
    for (left_t, right, extra), order in zip(members, orders):
        kept, sent = first_halves(left_t, right, order, extra)
        left = list(BITS)
        for step in range(3):
            kept, sent, left = halving(kept, sent, order[step:], left, step == 2)
        after.append(kept)
    return (after, left)


def finish(value, left, order):
    dim = left.index(order[0])
    kept, sent = (pick(value, dim, 0), pick(value, dim, 1))
    for step in range(3):
        kept, sent, left = halving(kept, sent, order[step:], left, False)
    return kept


def xor_order(left_t):
    width = left_t.shape[-1]
    value = left_t.reshape(4, 4, 4, DOWN_ROWS, width)
    me = lax.axis_index("dp")
    for dim, shift in enumerate((4, 2, 0)):
        mine = gray(me >> shift & 3)
        value = jnp.concatenate(
            [lax.dynamic_slice_in_dim(value, gray(mine ^ place), 1, dim) for place in range(4)],
            axis=dim,
        )
    return value


def body(
    inputs,
    starts,
    cotangent,
    w_query,
    w_key,
    w_value,
    w_output,
    w_gate,
    w_up,
    w_down,
    attn_gain,
    ffn_gain,
):
    section = lax.axis_index("section")
    micro, rows = starts.shape
    gains = jnp.concatenate([attn_gain, ffn_gain], axis=1)
    gain_row = jnp.pad(gains, ((0, 0), (0, D - gains.shape[1])))
    blank = jnp.zeros((1, D), bf16)
    slabs = (
        w_query[0],
        w_output[0],
        w_gate[0, :, :960],
        w_gate[0, :, 960:1920],
        w_up[0, :, :960],
        w_up[0, :, 960:1920],
        jnp.concatenate([w_gate[0, :, 1920:], w_key[0]], axis=1),
        jnp.concatenate([w_up[0, :, 1920:], w_value[0]], axis=1),
    )
    pieces = []
    for index, slab in enumerate(slabs):
        pieces += [slab, gain_row if index == 0 else blank]
    packed = jnp.concatenate(pieces + [w_down[0]], axis=0)[None]
    everything = lax.all_gather(packed, "dp", axis=0, tiled=True)

    def slab_of(index):
        part = everything[:, PADDED * index : PADDED * (index + 1)]
        return part.reshape(OWNERS * PADDED, D)

    mixed_gate, mixed_up = (slab_of(6), slab_of(7))
    all_gains = everything[:, SLOT, : 2 * SLOT].astype(f32)
    weights = (
        slab_of(0),
        mixed_gate[:, 640:],
        mixed_up[:, 640:],
        slab_of(1),
        jnp.concatenate([slab_of(2), slab_of(3), mixed_gate[:, :640]], axis=1),
        jnp.concatenate([slab_of(4), slab_of(5), mixed_up[:, :640]], axis=1),
        everything[:, 8 * PADDED :].reshape(FF, D),
        all_gains[:, :SLOT].reshape(D),
        all_gains[:, SLOT:].reshape(D),
    )
    spread = spread_matrix()
    mine = own_spread()
    geo = geometry(starts)
    first_in = inputs.reshape(micro * rows, D)
    top = cotangent.reshape(micro * rows, D)
    made, _ = forward(first_in, weights, geo, spread)
    arrived = lax.ppermute(made, "section", [(0, 1)])
    source = jnp.where(section == 0, first_in, arrived)
    result, saved = forward(source, weights, geo, spread)
    back, _ = backward(saved, top, weights, geo, spread)
    returned = lax.ppermute(back, "section", [(1, 0)])
    upstream = jnp.where(section == 1, top, returned)
    grad_rows, grads = backward(saved, upstream, weights, geo, spread)
    d3_low, dg, du, dm_low, dq, dk, dv, dattn, dffn = grads
    a, o, b, hidden = (saved[2], saved[8], saved[11], saved[14])
    a_t = blocks(dot_t(mine, a).astype(bf16), PADDED)
    o_t = blocks(dot_t(mine, o).astype(bf16), PADDED)
    b_t = blocks(dot_t(mine, b).astype(bf16), PADDED)
    hidden_t = blocks(xor_order(hidden.T), DOWN_ROWS)
    half = FF // 2
    outs = []
    for group, orders in enumerate(ORDERS):
        cut = slice(group * half, (group + 1) * half)
        down_cut = slice(0, 512) if group == 0 else slice(512, D)
        members = (
            (b_t, dg[:, cut], None),
            (b_t, du[:, cut], None),
            (hidden_t, d3_low[:, down_cut], None),
        )
        (gate_part, up_part, down_part), left = reduce_three(members, orders)
        pair = jnp.concatenate([gate_part, up_part], axis=-1)
        outs.append((finish(pair, left, orders[0][3:]), finish(down_part, left, orders[1][3:])))
    grad_gate = jnp.concatenate([outs[0][0][:SLOT, :half], outs[1][0][:SLOT, :half]], axis=1)
    grad_up = jnp.concatenate([outs[0][0][:SLOT, half:], outs[1][0][:SLOT, half:]], axis=1)
    grad_down = jnp.concatenate([outs[0][1], outs[1][1]], axis=1)
    owner = owner_of(jnp.arange(OWNERS, dtype=jnp.int32))
    choose = (owner[:, None] == jnp.arange(OWNERS, dtype=jnp.int32)[None, :]).astype(f32)
    both = jnp.concatenate([dattn.reshape(OWNERS, SLOT), dffn.reshape(OWNERS, SLOT)], axis=1)
    both = jnp.dot(choose, both, precision=lax.Precision.HIGHEST)
    extra = jnp.pad(both[:, None, :], ((0, 0), (SLOT, 0), (0, 512 - 2 * SLOT)))
    extra = extra.reshape((2,) * 6 + extra.shape[1:])
    dqkv = jnp.concatenate([dq, dk, dv], axis=1)
    cuts = (((0, 512), (512, 896), (0, 512)), ((896, 1280), (1280, 1600), (512, 960)))
    ends = []
    for group, orders in enumerate(ORDERS):
        (lo0, hi0), (lo1, hi1), (lo2, hi2) = cuts[group]
        members = (
            (a_t, dqkv[:, lo0:hi0], extra if group == 0 else None),
            (a_t, dqkv[:, lo1:hi1], None),
            (o_t, dm_low[:, lo2:hi2], None),
        )
        parts, left = reduce_three(members, orders)
        ends.append(finish(jnp.concatenate(parts, axis=-1), left, orders[2][3:]))
    dqkv_sum = jnp.concatenate([ends[0][:, :896], ends[1][:, :704]], axis=1)
    grad_output = jnp.concatenate([ends[0][:SLOT, 896:], ends[1][:SLOT, 704:]], axis=1)
    gain_sum = dqkv_sum[SLOT]
    return (
        result.reshape(1, micro, rows, D),
        grad_rows.reshape(1, micro, rows, D),
        dqkv_sum[None, :SLOT, :QD],
        dqkv_sum[None, :SLOT, QD : QD + KVD],
        dqkv_sum[None, :SLOT, QD + KVD :],
        grad_output[None],
        grad_gate[None],
        grad_up[None],
        grad_down[None],
        gain_sum[None, :SLOT],
        gain_sum[None, SLOT : 2 * SLOT],
    )


def solution(mesh):
    split = P("section", "dp", None)
    return jax.shard_map(
        body,
        mesh=mesh,
        in_specs=(P(None, "dp", None), P(None, "dp"), P(None, "dp", None))
        + (split,) * 7
        + (P("section", "dp"),) * 2,
        out_specs=(P("section", None, "dp", None),) * 2 + (split,) * 7 + (P("section", "dp"),) * 2,
        check_vma=False,
    )
```

profile of v0, /device:TPU:0, one launch (start us, length us, event | category | flops | bytes accessed | tf_op | source)
XLA Modules:
  0.0 695.9 jit_solution(18312639597677706957)
XLA Ops:
  11.1 18.6 %concatenate.104 = bf16[168,960]{1,0:T(8,128)(2,1)} concatenate(bf16[15,960]{1,0:T(8,128)(2,1)} %bitcast.888, bf16[1,960]{1,0:T(2,128)(2,1)S(1)} %fusion.272, bf16[15,960]{1,0:T(8,128)(2,1)} %bitcast.889, bf16[1,960]{1,0:T(2,128)(2,1)S(1)} %broadcast.365, bf16[15,960]{1,0:T(8,128)(2,1)S(1)} %get-tuple-element.178, bf16[1,960]{1,0:T(2,128)(2,1)S(1)} %broadcast.365, ...), dimensions={0} | concatenate | bytes 645120 | tf_op jit(solution)/shard_map/concatenate | solution.py:290
  40.9 112.3 %all-gather.3.cloned.1.call-done = bf16[10752,960]{1,0:T(8,128)(2,1)} async-done(((bf16[168,960]{1,0:T(8,128)(2,1)}), bf16[10752,960]{1,0:T(8,128)(2,1)}) %all-gather.3.cloned.1.call-update) | async-done | bytes 20643856 | tf_op jit(solution)/shard_map/all_gather | solution.py:291
  154.1 5.5 slice.1024
  159.6 11.7 %fusion.328 = (bf16[64,16,960]{2,1,0:T(8,128)(2,1)}, bf16[64,16,960]{2,1,0:T(8,128)(2,1)}, bf16[64,16,960]{2,1,0:T(8,128)(2,1)}, bf16[64,16,960]{2,1,0:T(8,128)(...) fusion(bf16[64,168,960]{2,1,0:T(8,128)(2,1)} %bitcast.821), kind=kLoop, calls=%fused_computation.648 | loop fusion | bytes 31457280 | tf_op jit(solution)/shard_map/slice | solution.py:294
  172.2 2.6 slice.1020
  175.8 2.3 fusion.86
  189.1 2.6 copy.130
  191.7 2.3 fusion.345
  201.5 2.6 fusion.337
  204.2 3.0 fusion.37
  207.1 2.3 copy.135
  211.4 4.6 multiply_reduce_fusion.7
  217.2 9.6 %concatenate.109 = bf16[1024,2560]{1,0:T(8,128)(2,1)} concatenate(bf16[1024,960]{1,0:T(8,128)(2,1)} %bitcast.847, bf16[1024,960]{1,0:T(8,128)(2,1)} %bitcast.846, bf16[1024,640]{1,0:T(8,128)(2,1)} %slice.1020), dimensions={1} | concatenate | bytes 10485760 | tf_op jit(solution)/shard_map/concatenate | solution.py:304
  226.8 2.2 convolution_convert_fusion.32
  231.4 9.6 %concatenate.110 = bf16[1024,2560]{1,0:T(8,128)(2,1)} concatenate(bf16[1024,960]{1,0:T(8,128)(2,1)} %bitcast.845, bf16[1024,960]{1,0:T(8,128)(2,1)} %bitcast.844, bf16[1024,640]{1,0:T(8,128)(2,1)S(1)} %slice.1023), dimensions={1} | concatenate | bytes 10485760 | tf_op jit(solution)/shard_map/concatenate | solution.py:305
  241.0 7.0 %fusion.42 = bf16[128,960]{0,1:T(8,128)(2,1)S(1)} fusion(f32[128,960]{0,1:T(8,128)} %get-tuple-element.159, bf16[2560,960]{1,0:T(8,128)(2,1)} %bitcast.822, bf16[128,1024]{1,0:T(8,128)(2,1)} %copy-done.67, bf16[1024,2560]{1,0:T(8,128)(2,1)} %concatenate.110, f32[128,2560]{1,0:T(8,128)} %fusion.346, f32[128]{0:T(128)S(1)} %mul.607), kind=kOutput, calls=%fused_computation.134 | convolution fusion | flops 1302568960 | bytes 12468736 | tf_op jit(solution)/shard_map/dot_general | solution.py:53
  249.9 5.4 fusion.349
  276.2 2.4 fusion.38
  281.1 4.1 convolution_convert_fusion.25
  285.2 3.3 multiply_reduce_fusion.6
  298.5 2.7 fusion.41
  307.5 4.1 convolution_convert_fusion.36
  312.8 2.3 fusion.50
  353.7 3.7 convolution_convert_fusion.35
  359.4 2.6 fusion.49
  374.3 2.6 fusion.352
  379.6 2.7 convolution_convert_fusion.10
  398.7 2.8 collective-permute-start.5
  412.9 2.6 convolution_convert_fusion.9
  415.5 2.5 convolution_convert_fusion.7
  421.1 2.5 convolution_convert_fusion.1
  431.8 4.3 pad_slice_fusion.1
  436.1 3.7 copy.174
  439.8 3.1 copy.176
  457.9 24.5 %collective-permute-done.18 = bf16[2,2,2,2,16,320]{5,4,2,3,0,1:T(8,128)(2,1)S(1)} collective-permute-done((bf16[2,2,2,2,16,320]{5,4,2,3,0,1:T(8,128)(2,1)S(1)}, bf16[2,2,2,2,16,320]{5,4,2,3,0,1:T(8,128)(2,1)S(1)}, u32[]{:S(2)}, u32[]{:S(2)}) %collective-permute-start.18) | collective-permute-done | bytes 163872 | tf_op jit(solution)/shard_map/ppermute | solution.py:215
  488.4 3.9 collective-permute-done.19
  494.7 3.2 collective-permute-done.15
  501.7 19.8 %collective-permute-done.7 = bf16[2,2,2,16,384]{4,3,2,1,0:T(8,128)(2,1)S(1)} collective-permute-done((bf16[2,2,2,16,384]{4,3,2,1,0:T(8,128)(2,1)S(1)}, bf16[2,2,2,16,384]{4,3,2,1,0:T(8,128)(2,1)S(1)}, u32[]{:S(2)}, u32[]{:S(2)}) %collective-permute-start.7) | collective-permute-done | bytes 98336 | tf_op jit(solution)/shard_map/ppermute | solution.py:215
  523.1 3.0 collective-permute-done.16
  529.2 4.4 collective-permute-done.3
  534.7 3.9 collective-permute-done.22
  541.7 3.6 collective-permute-done.10
  548.3 3.5 collective-permute-done.4
  554.9 3.2 collective-permute-done.23
  559.7 4.1 collective-permute-done.24
  565.8 3.3 collective-permute-done.25
  569.1 5.5 collective-permute-done.11
  576.2 4.1 collective-permute-done.12
  584.1 2.8 collective-permute-done.13
  590.3 2.2 collective-permute-start.45
  596.1 13.1 %collective-permute-done.29 = bf16[2,2,2,2,2,16,1280]{6,5,4,2,1,3,0:T(8,128)(2,1)S(1)} collective-permute-done((bf16[2,2,2,2,2,16,1280]{6,5,4,2,1,3,0:T(8,128)(2,1)S(1)}, bf16[2,2,2,2,2,16,1280]{6,5,4,2,1,3,0:T(8,128)(2,1)S(1)}, u32[]{:S(2)}, u32[]{:S(2)}) %collective-permute-start.29) | collective-permute-done | bytes 1310752 | tf_op jit(solution)/shard_map/ppermute | solution.py:215
  609.6 4.2 collective-permute-done.38
  618.7 2.6 collective-permute-start.46
  621.4 3.8 collective-permute-done.52
  628.9 5.2 collective-permute-done.53
  636.9 4.4 collective-permute-done.54
  641.2 2.4 collective-permute-start.31
  644.7 8.8 %collective-permute-done.55 = bf16[40,448]{1,0:T(8,128)(2,1)S(1)} collective-permute-done((bf16[40,448]{1,0:T(8,128)(2,1)S(1)}, bf16[40,448]{1,0:T(8,128)(2,1)S(1)}, u32[]{:S(2)}, u32[]{:S(2)}) %collective-permute-start.55) | collective-permute-done | bytes 35872 | tf_op jit(solution)/shard_map/ppermute | solution.py:215
  656.3 2.8 collective-permute-done.47
  660.7 3.2 collective-permute-done.48
  666.0 2.3 collective-permute-start.41
  669.2 5.2 collective-permute-done.41
  675.5 5.6 collective-permute-done.42
  682.5 4.4 collective-permute-done.43
  (593 shorter events, 259.9 us)
Async XLA Ops:
  7.2 146.0 %all-gather.3.cloned.1.call-start = ((), (), s32[]{:S(2)}) async-start(), calls=%async_computation | async-start | bytes 22364160 | tf_op jit(solution)/shard_map/all_gather | solution.py:291
  37.1 137.7 %copy-start.44 = (bf16[128,960]{0,1:T(8,128)(2,1)}, bf16[128,960]{0,1:T(8,128)(2,1)S(1)}, u32[]{:S(2)}) copy-start(bf16[128,960]{0,1:T(8,128)(2,1)S(1)} %copy.136) | copy-start | bytes 737284
  37.7 137.1 %copy-start.96 = (pred[1024]{0:T(1024)(128)(4,1)}, pred[1024]{0:T(1024)(128)(4,1)S(1)}, u32[]{:S(2)}) copy-start(pred[1024]{0:T(1024)(128)(4,1)S(1)} %get-tuple-element.180) | copy-start | bytes 3076
  37.7 137.1 %copy-start.101 = (pred[1024]{0:T(1024)(128)(4,1)}, pred[1024]{0:T(1024)(128)(4,1)S(1)}, u32[]{:S(2)}) copy-start(pred[1024]{0:T(1024)(128)(4,1)S(1)} %get-tuple-element.181) | copy-start | bytes 3076
  37.8 137.0 %copy-start.75 = (s32[1024]{0:T(1024)}, s32[1024]{0:T(1024)S(1)}, u32[]{:S(2)}) copy-start(s32[1024]{0:T(1024)S(1)} %get-tuple-element.185) | copy-start | bytes 12292
  37.8 312.4 %copy-start.73 = (s32[1024]{0:T(1024)}, s32[1024]{0:T(1024)S(1)}, u32[]{:S(2)}) copy-start(s32[1024]{0:T(1024)S(1)} %get-tuple-element.184) | copy-start | bytes 12292
  37.8 137.0 %copy-start.80 = (s32[1024]{0:T(1024)}, s32[1024]{0:T(1024)S(1)}, u32[]{:S(2)}) copy-start(s32[1024]{0:T(1024)S(1)} %get-tuple-element.182) | copy-start | bytes 12292
  37.8 137.0 %copy-start.85 = (s32[1024]{0:T(1024)}, s32[1024]{0:T(1024)S(1)}, u32[]{:S(2)}) copy-start(s32[1024]{0:T(1024)S(1)} %get-tuple-element.183) | copy-start | bytes 12292
  248.1 7.3 %collective-permute-start = (bf16[128,960]{0,1:T(8,128)(2,1)S(1)}, bf16[128,960]{0,1:T(8,128)(2,1)S(1)}, u32[]{:S(2)}, u32[]{:S(2)}) collective-permute-start(bf16[128,960]{0,1:T(8,128)(2,1)S(1)} %fusion.42), channel_id=1, source_target_pairs={{0,64},{1,65},{2,66},{3,67},{4,68},{5,69},{6,70},{7,71},{8,72},{9,... | collective-permute-start | bytes 737288 | tf_op jit(solution)/shard_map/ppermute | solution.py:316
  339.6 3.5 collective-permute-start.1
  398.7 54.5 %collective-permute-start.5 = (bf16[2,2,2,2,2,16,384]{6,5,4,2,1,3,0:T(8,128)(2,1)}, bf16[2,2,2,2,2,16,384]{6,5,4,2,1,3,0:T(8,128)(2,1)}, u32[]{:S(2)}, u32[]{:S(2)}) collective-permute-start(bf16[2,2,2,2,2,16,384]{6,5,4,2,1,3,0:T(8,128)(2,1)} %convolution_convert_fusion.22), channel_id=1, source_target_pairs={{0,12},{1,13},{2,14},{3,15},{4,8},{5,9},{6,10},{7,11},{8,4},{9,5},... | collective-permute-start | bytes 1179656 | tf_op jit(solution)/shard_map/ppermute | solution.py:215
  401.5 48.7 %collective-permute-start.14 = (bf16[2,2,2,2,2,16,384]{6,5,1,3,0,4,2:T(8,128)(2,1)}, bf16[2,2,2,2,2,16,384]{6,5,1,3,0,4,2:T(8,128)(2,1)}, u32[]{:S(2)}, u32[]{:S(2)}) collective-permute-start(bf16[2,2,2,2,2,16,384]{6,5,1,3,0,4,2:T(8,128)(2,1)} %convolution_convert_fusion.20), channel_id=1, source_target_pairs={{0,16},{1,17},{2,18},{3,19},{4,20},{5,21},{6,22},{7,23},{8,24},{9,... | collective-permute-start | bytes 1179656 | tf_op jit(solution)/shard_map/ppermute | solution.py:215
  404.0 43.2 %collective-permute-start.17 = (bf16[2,2,2,2,2,16,320]{6,5,2,3,0,1,4:T(8,128)(2,1)}, bf16[2,2,2,2,2,16,320]{6,5,2,3,0,1,4:T(8,128)(2,1)}, u32[]{:S(2)}, u32[]{:S(2)}) collective-permute-start(bf16[2,2,2,2,2,16,320]{6,5,2,3,0,1,4:T(8,128)(2,1)} %convolution_convert_fusion.18), channel_id=1, source_target_pairs={{0,4},{1,5},{2,6},{3,7},{4,0},{5,1},{6,2},{7,3},{8,12},{9,13},{10,... | collective-permute-start | bytes 983048 | tf_op jit(solution)/shard_map/ppermute | solution.py:215
  411.2 73.0 %collective-permute-start.8 = (bf16[2,2,2,2,2,16,512]{6,5,4,3,1,2,0:T(8,128)(2,1)}, bf16[2,2,2,2,2,16,512]{6,5,4,3,1,2,0:T(8,128)(2,1)}, u32[]{:S(2)}, u32[]{:S(2)}) collective-permute-start(bf16[2,2,2,2,2,16,512]{6,5,4,3,1,2,0:T(8,128)(2,1)} %convolution_convert_fusion.14), channel_id=1, source_target_pairs={{0,3},{1,2},{2,1},{3,0},{4,7},{5,6},{6,5},{7,4},{8,11},{9,10},{10,... | collective-permute-start | bytes 1572872 | tf_op jit(solution)/shard_map/ppermute | solution.py:215
  412.7 43.9 %collective-permute-start.20 = (bf16[2,2,2,2,2,16,448]{6,5,2,4,0,3,1:T(8,128)(2,1)}, bf16[2,2,2,2,2,16,448]{6,5,2,4,0,3,1:T(8,128)(2,1)}, u32[]{:S(2)}, u32[]{:S(2)}) collective-permute-start(bf16[2,2,2,2,2,16,448]{6,5,2,4,0,3,1:T(8,128)(2,1)} %convolution_convert_fusion.12), channel_id=1, source_target_pairs={{0,1},{1,0},{2,3},{3,2},{4,5},{5,4},{6,7},{7,6},{8,9},{9,8},{10,11... | collective-permute-start | bytes 1376264 | tf_op jit(solution)/shard_map/ppermute | solution.py:215
  447.3 134.9 %collective-permute-start.50 = (bf16[2,2,2,2,2,40,448]{6,5,4,0,2,3,1:T(8,128)(2,1)}, bf16[2,2,2,2,2,40,448]{6,5,4,0,2,3,1:T(8,128)(2,1)}, u32[]{:S(2)}, u32[]{:S(2)}) collective-permute-start(bf16[2,2,2,2,2,40,448]{6,5,4,0,2,3,1:T(8,128)(2,1)} %convolution_convert_fusion.8), channel_id=1, source_target_pairs={{0,1},{1,0},{2,3},{3,2},{4,5},{5,4},{6,7},{7,6},{8,9},{9,8},{10,11... | collective-permute-start | bytes 3440648 | tf_op jit(solution)/shard_map/ppermute | solution.py:215
  450.3 138.6 %collective-permute-start.44 = (bf16[2,2,2,2,2,40,512]{6,5,4,3,1,2,0:T(8,128)(2,1)}, bf16[2,2,2,2,2,40,512]{6,5,4,3,1,2,0:T(8,128)(2,1)}, u32[]{:S(2)}, u32[]{:S(2)}) collective-permute-start(bf16[2,2,2,2,2,40,512]{6,5,4,3,1,2,0:T(8,128)(2,1)} %convolution_convert_fusion.10), channel_id=1, source_target_pairs={{0,3},{1,2},{2,1},{3,0},{4,7},{5,6},{6,5},{7,4},{8,11},{9,10},{10,... | collective-permute-start | bytes 3932168 | tf_op jit(solution)/shard_map/ppermute | solution.py:215
  453.2 34.3 %collective-permute-start.2 = (bf16[2,2,2,2,2,16,512]{6,5,4,2,0,3,1:T(8,128)(2,1)S(1)}, bf16[2,2,2,2,2,16,512]{6,5,4,2,0,3,1:T(8,128)(2,1)S(1)}, u32[]{:S(2)}, u32[]{:S(2)}) collective-permute-start(bf16[2,2,2,2,2,16,512]{6,5,4,2,0,3,1:T(8,128)(2,1)S(1)} %fusion.34), channel_id=1, source_target_pairs={{0,48},{1,49},{2,50},{3,51},{4,52},{5,53},{6,54},{7,55},{8,56},{9,... | collective-permute-start | bytes 1572872 | tf_op jit(solution)/shard_map/ppermute | solution.py:215
  456.5 25.9 %collective-permute-start.18 = (bf16[2,2,2,2,16,320]{5,4,2,3,0,1:T(8,128)(2,1)S(1)}, bf16[2,2,2,2,16,320]{5,4,2,3,0,1:T(8,128)(2,1)S(1)}, u32[]{:S(2)}, u32[]{:S(2)}) collective-permute-start(bf16[2,2,2,2,16,320]{5,4,2,3,0,1:T(8,128)(2,1)S(1)} %get-tuple-element.78), channel_id=1, source_target_pairs={{0,1},{1,0},{2,3},{3,2},{4,5},{5,4},{6,7},{7,6},{8,9},{9,8},{10,11... | collective-permute-start | bytes 491528 | tf_op jit(solution)/shard_map/ppermute | solution.py:215
  482.4 107.9 %collective-permute-start.26 = (bf16[2,2,2,2,2,16,1280]{6,5,4,2,0,3,1:T(8,128)(2,1)}, bf16[2,2,2,2,2,16,1280]{6,5,4,2,0,3,1:T(8,128)(2,1)}, u32[]{:S(2)}, u32[]{:S(2)}) collective-permute-start(bf16[2,2,2,2,2,16,1280]{6,5,4,2,0,3,1:T(8,128)(2,1)} %convolution_convert_fusion.6), channel_id=1, source_target_pairs={{0,48},{1,49},{2,50},{3,51},{4,52},{5,53},{6,54},{7,55},{8,56},{9,... | collective-permute-start | bytes 3932168 | tf_op jit(solution)/shard_map/ppermute | solution.py:215
  484.2 9.9 %collective-permute-start.6 = (bf16[2,2,2,2,16,384]{5,4,3,2,1,0:T(8,128)(2,1)S(1)}, bf16[2,2,2,2,16,384]{5,4,3,2,1,0:T(8,128)(2,1)S(1)}, u32[]{:S(2)}, u32[]{:S(2)}) collective-permute-start(bf16[2,2,2,2,16,384]{5,4,3,2,1,0:T(8,128)(2,1)S(1)} %get-tuple-element.76), channel_id=1, source_target_pairs={{0,3},{1,2},{2,1},{3,0},{4,7},{5,6},{6,5},{7,4},{8,11},{9,10},{10,... | collective-permute-start | bytes 589832 | tf_op jit(solution)/shard_map/ppermute | solution.py:215
  487.6 4.7 collective-permute-start.19
  492.3 5.7 collective-permute-start.15
  494.0 6.5 collective-permute-start.21
  497.9 30.6 %collective-permute-start.9 = (bf16[2,2,2,2,16,512]{5,4,3,2,0,1:T(8,128)(2,1)S(1)}, bf16[2,2,2,2,16,512]{5,4,3,2,0,1:T(8,128)(2,1)S(1)}, u32[]{:S(2)}, u32[]{:S(2)}) collective-permute-start(bf16[2,2,2,2,16,512]{5,4,3,2,0,1:T(8,128)(2,1)S(1)} %get-tuple-element.60), channel_id=1, source_target_pairs={{0,48},{1,49},{2,50},{3,51},{4,52},{5,53},{6,54},{7,55},{8,56},{9,... | collective-permute-start | bytes 786440 | tf_op jit(solution)/shard_map/ppermute | solution.py:215
  500.5 20.9 %collective-permute-start.7 = (bf16[2,2,2,16,384]{4,3,2,1,0:T(8,128)(2,1)S(1)}, bf16[2,2,2,16,384]{4,3,2,1,0:T(8,128)(2,1)S(1)}, u32[]{:S(2)}, u32[]{:S(2)}) collective-permute-start(bf16[2,2,2,16,384]{4,3,2,1,0:T(8,128)(2,1)S(1)} %fusion.229), channel_id=1, source_target_pairs={{0,48},{1,49},{2,50},{3,51},{4,52},{5,53},{6,54},{7,55},{8,56},{9,... | collective-permute-start | bytes 294920 | tf_op jit(solution)/shard_map/ppermute | solution.py:215
  521.4 4.6 collective-permute-start.16
  526.1 7.6 %collective-permute-start.3 = (bf16[2,2,2,2,16,512]{5,4,3,2,1,0:T(8,128)(2,1)S(1)}, bf16[2,2,2,2,16,512]{5,4,3,2,1,0:T(8,128)(2,1)S(1)}, u32[]{:S(2)}, u32[]{:S(2)}) collective-permute-start(bf16[2,2,2,2,16,512]{5,4,3,2,1,0:T(8,128)(2,1)S(1)} %fusion.147), channel_id=1, source_target_pairs={{0,12},{1,13},{2,14},{3,15},{4,8},{5,9},{6,10},{7,11},{8,4},{9,5},... | collective-permute-start | bytes 786440 | tf_op jit(solution)/shard_map/ppermute | solution.py:215
  528.5 65.3 %collective-permute-start.35 = (bf16[2,2,2,2,2,16,1280]{6,5,3,1,0,4,2:T(8,128)(2,1)}, bf16[2,2,2,2,2,16,1280]{6,5,3,1,0,4,2:T(8,128)(2,1)}, u32[]{:S(2)}, u32[]{:S(2)}) collective-permute-start(bf16[2,2,2,2,2,16,1280]{6,5,3,1,0,4,2:T(8,128)(2,1)} %convolution_convert_fusion.2), channel_id=1, source_target_pairs={{0,16},{1,17},{2,18},{3,19},{4,20},{5,21},{6,22},{7,23},{8,24},{9,... | collective-permute-start | bytes 3932168 | tf_op jit(solution)/shard_map/ppermute | solution.py:215
  533.6 5.0 collective-permute-start.22
  538.6 6.7 collective-permute-start.10
  545.3 6.5 collective-permute-start.4
  551.8 6.4 collective-permute-start.23
  558.2 5.6 collective-permute-start.24
  563.9 5.2 collective-permute-start.25
  569.1 5.5 collective-permute-start.11
  574.7 5.6 collective-permute-start.12
  580.3 28.9 %collective-permute-start.29 = (bf16[2,2,2,2,2,16,1280]{6,5,4,2,1,3,0:T(8,128)(2,1)S(1)}, bf16[2,2,2,2,2,16,1280]{6,5,4,2,1,3,0:T(8,128)(2,1)S(1)}, u32[]{:S(2)}, u32[]{:S(2)}) collective-permute-start(bf16[2,2,2,2,2,16,1280]{6,5,4,2,1,3,0:T(8,128)(2,1)S(1)} %copy-done.36), channel_id=1, source_target_pairs={{0,12},{1,13},{2,14},{3,15},{4,8},{5,9},{6,10},{7,11},{8,4},{9,5},... | collective-permute-start | bytes 3932168 | tf_op jit(solution)/shard_map/ppermute | solution.py:215
  582.2 4.7 collective-permute-start.13
  586.9 26.9 %collective-permute-start.38 = (bf16[2,2,2,2,2,16,1280]{6,5,3,2,0,1,4:T(8,128)(2,1)S(1)}, bf16[2,2,2,2,2,16,1280]{6,5,3,2,0,1,4:T(8,128)(2,1)S(1)}, u32[]{:S(2)}, u32[]{:S(2)}) collective-permute-start(bf16[2,2,2,2,2,16,1280]{6,5,3,2,0,1,4:T(8,128)(2,1)S(1)} %copy-done.35), channel_id=1, source_target_pairs={{0,4},{1,5},{2,6},{3,7},{4,0},{5,1},{6,2},{7,3},{8,12},{9,13},{10,... | collective-permute-start | bytes 3932168 | tf_op jit(solution)/shard_map/ppermute | solution.py:215
  588.9 29.0 %collective-permute-start.51 = (bf16[2,2,2,2,40,448]{5,4,3,0,1,2:T(8,128)(2,1)S(1)}, bf16[2,2,2,2,40,448]{5,4,3,0,1,2:T(8,128)(2,1)S(1)}, u32[]{:S(2)}, u32[]{:S(2)}) collective-permute-start(bf16[2,2,2,2,40,448]{5,4,3,0,1,2:T(8,128)(2,1)S(1)} %get-tuple-element.50), channel_id=1, source_target_pairs={{0,16},{1,17},{2,18},{3,19},{4,20},{5,21},{6,22},{7,23},{8,24},{9,... | collective-permute-start | bytes 1720328 | tf_op jit(solution)/shard_map/ppermute | solution.py:215
  590.3 27.8 %collective-permute-start.45 = (bf16[2,2,2,2,40,512]{5,4,3,2,1,0:T(8,128)(2,1)S(1)}, bf16[2,2,2,2,40,512]{5,4,3,2,1,0:T(8,128)(2,1)S(1)}, u32[]{:S(2)}, u32[]{:S(2)}) collective-permute-start(bf16[2,2,2,2,40,512]{5,4,3,2,1,0:T(8,128)(2,1)S(1)} %fusion.68), channel_id=1, source_target_pairs={{0,48},{1,49},{2,50},{3,51},{4,52},{5,53},{6,54},{7,55},{8,56},{9,... | collective-permute-start | bytes 1966088 | tf_op jit(solution)/shard_map/ppermute | solution.py:215
  593.8 24.9 %collective-permute-start.27 = (bf16[2,2,2,2,16,1280]{5,4,3,2,1,0:T(8,128)(2,1)S(1)}, bf16[2,2,2,2,16,1280]{5,4,3,2,1,0:T(8,128)(2,1)S(1)}, u32[]{:S(2)}, u32[]{:S(2)}) collective-permute-start(bf16[2,2,2,2,16,1280]{5,4,3,2,1,0:T(8,128)(2,1)S(1)} %fusion.67), channel_id=1, source_target_pairs={{0,12},{1,13},{2,14},{3,15},{4,8},{5,9},{6,10},{7,11},{8,4},{9,5},... | collective-permute-start | bytes 1966088 | tf_op jit(solution)/shard_map/ppermute | solution.py:215
  609.2 18.2 %collective-permute-start.36 = (bf16[2,2,2,2,16,1280]{5,4,2,1,0,3:T(8,128)(2,1)S(1)}, bf16[2,2,2,2,16,1280]{5,4,2,1,0,3:T(8,128)(2,1)S(1)}, u32[]{:S(2)}, u32[]{:S(2)}) collective-permute-start(bf16[2,2,2,2,16,1280]{5,4,2,1,0,3:T(8,128)(2,1)S(1)} %get-tuple-element.56), channel_id=1, source_target_pairs={{0,4},{1,5},{2,6},{3,7},{4,0},{5,1},{6,2},{7,3},{8,12},{9,13},{10,... | collective-permute-start | bytes 1966088 | tf_op jit(solution)/shard_map/ppermute | solution.py:215
  613.8 21.7 %collective-permute-start.30 = (bf16[2,2,2,2,16,1280]{5,4,3,2,1,0:T(8,128)(2,1)S(1)}, bf16[2,2,2,2,16,1280]{5,4,3,2,1,0:T(8,128)(2,1)S(1)}, u32[]{:S(2)}, u32[]{:S(2)}) collective-permute-start(bf16[2,2,2,2,16,1280]{5,4,3,2,1,0:T(8,128)(2,1)S(1)} %get-tuple-element.52), channel_id=1, source_target_pairs={{0,3},{1,2},{2,1},{3,0},{4,7},{5,6},{6,5},{7,4},{8,11},{9,10},{10,... | collective-permute-start | bytes 1966088 | tf_op jit(solution)/shard_map/ppermute | solution.py:215
  617.9 25.8 %collective-permute-start.39 = (bf16[2,2,2,2,16,1280]{5,4,3,2,0,1:T(8,128)(2,1)S(1)}, bf16[2,2,2,2,16,1280]{5,4,3,2,0,1:T(8,128)(2,1)S(1)}, u32[]{:S(2)}, u32[]{:S(2)}) collective-permute-start(bf16[2,2,2,2,16,1280]{5,4,3,2,0,1:T(8,128)(2,1)S(1)} %get-tuple-element.54), channel_id=1, source_target_pairs={{0,1},{1,0},{2,3},{3,2},{4,5},{5,4},{6,7},{7,6},{8,9},{9,8},{10,11... | collective-permute-start | bytes 1966088 | tf_op jit(solution)/shard_map/ppermute | solution.py:215
  618.1 7.2 %collective-permute-start.52 = (bf16[2,2,2,40,448]{4,3,2,0,1:T(8,128)(2,1)S(1)}, bf16[2,2,2,40,448]{4,3,2,0,1:T(8,128)(2,1)S(1)}, u32[]{:S(2)}, u32[]{:S(2)}) collective-permute-start(bf16[2,2,2,40,448]{4,3,2,0,1:T(8,128)(2,1)S(1)} %fusion.122), channel_id=1, source_target_pairs={{0,4},{1,5},{2,6},{3,7},{4,0},{5,1},{6,2},{7,3},{8,12},{9,13},{10,... | collective-permute-start | bytes 860168 | tf_op jit(solution)/shard_map/ppermute | solution.py:215
  618.7 34.8 %collective-permute-start.46 = (bf16[2,2,2,40,512]{4,3,2,1,0:T(8,128)(2,1)S(1)}, bf16[2,2,2,40,512]{4,3,2,1,0:T(8,128)(2,1)S(1)}, u32[]{:S(2)}, u32[]{:S(2)}) collective-permute-start(bf16[2,2,2,40,512]{4,3,2,1,0:T(8,128)(2,1)S(1)} %fusion.126), channel_id=1, source_target_pairs={{0,12},{1,13},{2,14},{3,15},{4,8},{5,9},{6,10},{7,11},{8,4},{9,5},... | collective-permute-start | bytes 983048 | tf_op jit(solution)/shard_map/ppermute | solution.py:215
  625.2 28.5 %collective-permute-start.28 = (bf16[2,2,2,16,1280]{4,3,2,1,0:T(8,128)(2,1)S(1)}, bf16[2,2,2,16,1280]{4,3,2,1,0:T(8,128)(2,1)S(1)}, u32[]{:S(2)}, u32[]{:S(2)}) collective-permute-start(bf16[2,2,2,16,1280]{4,3,2,1,0:T(8,128)(2,1)S(1)} %fusion.123), channel_id=1, source_target_pairs={{0,3},{1,2},{2,1},{3,0},{4,7},{5,6},{6,5},{7,4},{8,11},{9,10},{10,... | collective-permute-start | bytes 983048 | tf_op jit(solution)/shard_map/ppermute | solution.py:215
  627.4 6.6 collective-permute-start.53
  634.0 22.1 %collective-permute-start.37 = (bf16[2,2,2,16,1280]{4,3,2,1,0:T(8,128)(2,1)S(1)}, bf16[2,2,2,16,1280]{4,3,2,1,0:T(8,128)(2,1)S(1)}, u32[]{:S(2)}, u32[]{:S(2)}) collective-permute-start(bf16[2,2,2,16,1280]{4,3,2,1,0:T(8,128)(2,1)S(1)} %fusion.117), channel_id=1, source_target_pairs={{0,1},{1,0},{2,3},{3,2},{4,5},{5,4},{6,7},{7,6},{8,9},{9,8},{10,11... | collective-permute-start | bytes 983048 | tf_op jit(solution)/shard_map/ppermute | solution.py:215
  635.5 5.7 collective-permute-start.54
  641.2 12.7 %collective-permute-start.31 = (bf16[2,2,2,16,1280]{4,3,2,1,0:T(8,128)(2,1)S(1)}, bf16[2,2,2,16,1280]{4,3,2,1,0:T(8,128)(2,1)S(1)}, u32[]{:S(2)}, u32[]{:S(2)}) collective-permute-start(bf16[2,2,2,16,1280]{4,3,2,1,0:T(8,128)(2,1)S(1)} %fusion.125), channel_id=1, source_target_pairs={{0,48},{1,49},{2,50},{3,51},{4,52},{5,53},{6,54},{7,55},{8,56},{9,... | collective-permute-start | bytes 983048 | tf_op jit(solution)/shard_map/ppermute | solution.py:215
  643.7 9.8 %collective-permute-start.55 = (bf16[40,448]{1,0:T(8,128)(2,1)S(1)}, bf16[40,448]{1,0:T(8,128)(2,1)S(1)}, u32[]{:S(2)}, u32[]{:S(2)}) collective-permute-start(bf16[40,448]{1,0:T(8,128)(2,1)S(1)} %fusion.257), channel_id=1, source_target_pairs={{0,48},{1,49},{2,50},{3,51},{4,52},{5,53},{6,54},{7,55},{8,56},{9,... | collective-permute-start | bytes 107528 | tf_op jit(solution)/shard_map/ppermute | solution.py:215
  653.5 7.1 %collective-permute-start.40 = (bf16[2,2,2,16,1280]{4,3,2,1,0:T(8,128)(2,1)S(1)}, bf16[2,2,2,16,1280]{4,3,2,1,0:T(8,128)(2,1)S(1)}, u32[]{:S(2)}, u32[]{:S(2)}) collective-permute-start(bf16[2,2,2,16,1280]{4,3,2,1,0:T(8,128)(2,1)S(1)} %fusion.119), channel_id=1, source_target_pairs={{0,16},{1,17},{2,18},{3,19},{4,20},{5,21},{6,22},{7,23},{8,24},{9,... | collective-permute-start | bytes 983048 | tf_op jit(solution)/shard_map/ppermute | solution.py:215
  653.7 5.4 collective-permute-start.47
  654.1 14.9 %collective-permute-start.32 = (bf16[2,2,16,2560]{3,2,1,0:T(8,128)(2,1)S(1)}, bf16[2,2,16,2560]{3,2,1,0:T(8,128)(2,1)S(1)}, u32[]{:S(2)}, u32[]{:S(2)}) collective-permute-start(bf16[2,2,16,2560]{3,2,1,0:T(8,128)(2,1)S(1)} %fusion.130), channel_id=1, source_target_pairs={{0,16},{1,17},{2,18},{3,19},{4,20},{5,21},{6,22},{7,23},{8,24},{9,... | collective-permute-start | bytes 983048 | tf_op jit(solution)/shard_map/ppermute | solution.py:215
  659.1 4.8 collective-permute-start.48
  663.9 4.4 collective-permute-start.49
  666.0 8.4 %collective-permute-start.41 = (bf16[2,2,16,2560]{3,2,1,0:T(8,128)(2,1)S(1)}, bf16[2,2,16,2560]{3,2,1,0:T(8,128)(2,1)S(1)}, u32[]{:S(2)}, u32[]{:S(2)}) collective-permute-start(bf16[2,2,16,2560]{3,2,1,0:T(8,128)(2,1)S(1)} %fusion.128), channel_id=1, source_target_pairs={{0,48},{1,49},{2,50},{3,51},{4,52},{5,53},{6,54},{7,55},{8,56},{9,... | collective-permute-start | bytes 983048 | tf_op jit(solution)/shard_map/ppermute | solution.py:215
  669.1 6.3 collective-permute-start.33
  674.5 6.6 collective-permute-start.42
  675.4 7.0 %collective-permute-start.34 = (bf16[16,2560]{1,0:T(8,128)(2,1)S(1)}, bf16[16,2560]{1,0:T(8,128)(2,1)S(1)}, u32[]{:S(2)}, u32[]{:S(2)}) collective-permute-start(bf16[16,2560]{1,0:T(8,128)(2,1)S(1)} %fusion.232), channel_id=1, source_target_pairs={{0,1},{1,0},{2,3},{3,2},{4,5},{5,4},{6,7},{7,6},{8,9},{9,8},{10,11... | collective-permute-start | bytes 245768 | tf_op jit(solution)/shard_map/ppermute | solution.py:215
  681.1 5.7 collective-permute-start.43
  (115 other events, 1205.5 us)
Sparse Core Ops, SparseCore 0:
  29.8 123.3 all-gather.2
where the time goes:
time: 709 us; the launch traced here: 696 us
  waiting for transfers between devices  268 us (38%)
  local copies, waits for them, and re-layouts  152 us (21%)
  matrix products  147 us (21%)
  starting transfers between devices  66.3 us (9%)
  other arithmetic  45.4 us (6%)
  between operations  17 us (2%)
    ppermute x54, waiting for transfers between devices, halving(): arrived = lax.ppermute(sent, 'dp', partner_pairs(bit))  156 us
    all_gather x1, waiting for transfers between devices, body(): everything = lax.all_gather(packed, 'dp', axis=0, tiled=True)  112 us
    dot_general x41, matrix products, dot(): return jnp.dot(left, right, preferred_element_type=f32)  78.1 us
    ppermute x54, starting transfers between devices, halving(): arrived = lax.ppermute(sent, 'dp', partner_pairs(bit))  62.5 us
    dot_general x25, matrix products, dot_t(): lax.dot_general(left, right, (((1,), (1,)), ((), ())), preferred_element_...  47.5 us
    concatenate x1, local copies, waits for them, and re-layouts, body(): packed = jnp.concatenate(pieces + [w_down[0]], axis=0)[None]  18.6 us
    convert_element_type x39, other arithmetic, halving(): return (next_kept.astype(bf16), next_sent.astype(bf16), left)  17.7 us
  transfers between devices with their start and end apart: 57, of which 30 were waited for; matrix products, arithmetic and copies ran while one was open for 12% of the time, Pallas kernels for 0%

commit v1 on v0

--- a/solution.py
+++ b/solution.py
@@ -288,7 +288,10 @@
     for index, slab in enumerate(slabs):
         pieces += [slab, gain_row if index == 0 else blank]
     packed = jnp.concatenate(pieces + [w_down[0]], axis=0)[None]
-    everything = lax.all_gather(packed, "dp", axis=0, tiled=True)
+    size = lax.axis_size("dp")
+    shards = jnp.stack([packed for _ in range(size)])
+    shards = lax.all_to_all(shards, "dp", split_axis=0, concat_axis=0)
+    everything = jnp.concatenate(shards, axis=0)
 
     def slab_of(index):
         part = everything[:, PADDED * index : PADDED * (index + 1)]

time: 709 us -> 1080 us (1.52)
  waiting for transfers between devices: 268 us -> 507 us
  local copies, waits for them, and re-layouts: 152 us -> 246 us
  starting transfers between devices: 66.3 us -> 114 us
  between operations: 17 us -> 3.67 us
    all_to_all x0 -> x1, waiting for transfers between devices: none -> 341 us  [body(): shards = lax.all_to_all(shards, 'dp', split_axis=0, concat_axis=0)]
    all_gather x1 -> x0, waiting for transfers between devices: 112 us -> none  [body(): everything = lax.all_gather(packed, 'dp', axis=0, tiled=True)]
    slice x1 -> x9, local copies, waits for them, and re-layouts: 11.7 us -> 66 us  [slab_of(): part = everything[:, PADDED * index:PADDED * (index + 1)]]
    all_to_all x0 -> x1, local copies, waits for them, and re-layouts: none -> 43 us  [body(): shards = lax.all_to_all(shards, 'dp', split_axis=0, concat_axis=0)]
    ppermute x54, starting transfers between devices: 62.5 us -> 98.8 us  [halving(): arrived = lax.ppermute(sent, 'dp', partner_pairs(bit))]
    concatenate x1, local copies, waits for them, and re-layouts: 18.6 us -> 2.62 us  [body(): packed = jnp.concatenate(pieces + [w_down[0]], axis=0)[None]]
    slice x1 -> x2, local copies, waits for them, and re-layouts: 5.48 us -> 20.3 us  [body(): everything[:, 8 * PADDED:].reshape(FF, D)]
    all_to_all x0 -> x1, starting transfers between devices: none -> 11.9 us  [body(): shards = lax.all_to_all(shards, 'dp', split_axis=0, concat_axis=0)]
  transfers between devices with their start and end apart: 57 -> 57, of which waited for: 30 -> 35; matrix products, arithmetic and copies ran while one was open for 12% -> 9% of each run, Pallas kernels for 0% -> 0%
where the time goes in v1:
time: 1080 us; the launch traced here: 1070 us
  waiting for transfers between devices  507 us (47%)
  local copies, waits for them, and re-layouts  246 us (23%)
  matrix products  156 us (14%)
  starting transfers between devices  114 us (11%)
  other arithmetic  40.9 us (4%)
    all_to_all x1, waiting for transfers between devices, body(): shards = lax.all_to_all(shards, 'dp', split_axis=0, concat_axis=0)  341 us
    ppermute x54, waiting for transfers between devices, halving(): arrived = lax.ppermute(sent, 'dp', partner_pairs(bit))  166 us
    ppermute x54, starting transfers between devices, halving(): arrived = lax.ppermute(sent, 'dp', partner_pairs(bit))  98.8 us
    dot_general x41, matrix products, dot(): return jnp.dot(left, right, preferred_element_type=f32)  85 us
    slice x9, local copies, waits for them, and re-layouts, slab_of(): part = everything[:, PADDED * index:PADDED * (index + 1)]  66 us
    dot_general x25, matrix products, dot_t(): lax.dot_general(left, right, (((1,), (1,)), ((), ())), preferred_element_...  50.3 us
    all_to_all x1, local copies, waits for them, and re-layouts, body(): shards = lax.all_to_all(shards, 'dp', split_axis=0, concat_axis=0)  43 us
  transfers between devices with their start and end apart: 57, of which 35 were waited for; matrix products, arithmetic and copies ran while one was open for 9% of the time, Pallas kernels for 0%

profile of v1, /device:TPU:0, one launch (start us, length us, event | category | flops | bytes accessed | tf_op | source)
XLA Modules:
  0.0 1067.3 jit_solution(8258199018668543564)
XLA Ops:
  7.2 7.6 stack.3
  14.8 11.9 %all-to-all-start = ((bf16[64,1,168,960]{3,2,1,0:T(8,128)(2,1)}), bf16[64,1,168,960]{3,2,1,0:T(8,128)(2,1)}, u32[]{:S(2)}, u32[]{:S(2)}) async-start(bf16[64,1,168,960]{3,2,1,0:T(8,128)(2,1)} %stack.3), calls=%async_computation | async-start | bytes 44040192 | tf_op jit(solution)/shard_map/all_to_all | solution.py:293
  34.9 341.0 %all-to-all-done = bf16[64,1,168,960]{3,2,1,0:T(8,128)(2,1)} async-done(((bf16[64,1,168,960]{3,2,1,0:T(8,128)(2,1)}), bf16[64,1,168,960]{3,2,1,0:T(8,128)(2,1)}, u32[]{:S(2)}, u32[]{:S(2)}) %all-to-all-start) | async-done | bytes 20643872 | tf_op jit(solution)/shard_map/all_to_all | solution.py:293
  375.9 43.0 %copy.258 = bf16[64,1,168,960]{0,3,2,1:T(8,128)(2,1)} copy(bf16[64,1,168,960]{3,2,1,0:T(8,128)(2,1)} %all-to-all-done) | data formatting | bytes 41287680 | tf_op jit(solution)/shard_map/all_to_all | solution.py:293
  419.6 23.8 %fusion.328 = (bf16[64,16,960]{0,2,1:T(8,128)(2,1)}, bf16[64,16,960]{0,2,1:T(8,128)(2,1)}, bf16[64,16,960]{0,2,1:T(8,128)(2,1)}, bf16[64,16,960]{0,2,1:T(8,128)(...) fusion(bf16[64,168,960]{0,2,1:T(8,128)(2,1)} %bitcast.813), kind=kLoop, calls=%fused_computation.648 | loop fusion | bytes 31457280 | tf_op jit(solution)/shard_map/slice | solution.py:297
  443.6 4.7 copy.261
  451.9 4.6 copy.260
  459.9 8.2 slice.1024
  472.8 4.6 copy.266
  493.5 3.0 fusion.37
  500.8 5.7 copy.273
  506.4 4.5 multiply_reduce_fusion.7
  513.8 5.7 copy.275
  519.4 5.7 copy.276
  525.1 5.6 copy.277
  530.8 5.6 copy.278
  536.4 12.1 %copy.279 = bf16[64,40,960]{2,1,0:T(8,128)(2,1)} copy(bf16[64,40,960]{0,2,1:T(8,128)(2,1)} %slice.1024) | data formatting | bytes 9830400 | tf_op jit(solution)/shard_map/slice | solution.py:309
  551.3 9.2 concatenate.109
  560.5 4.6 fusion.346
  565.1 9.3 concatenate.110
  574.3 7.0 fusion.42
  583.3 5.4 fusion.349
  612.1 3.3 multiply_reduce_fusion.6
  616.4 3.5 fusion.348
  620.0 5.0 fusion.27
  631.6 3.9 convolution_convert_fusion.36
  648.4 3.1 convolution_convert_fusion.25
  686.2 4.8 multiply_convert_fusion
  698.5 3.7 convolution_convert_fusion.35
  720.5 26.4 %collective-permute-start.44 = (bf16[2,2,2,2,2,40,512]{6,5,4,3,1,2,0:T(8,128)(2,1)}, bf16[2,2,2,2,2,40,512]{6,5,4,3,1,2,0:T(8,128)(2,1)}, u32[]{:S(2)}, u32[]{:S(2)}) collective-permute-start(bf16[2,2,2,2,2,40,512]{6,5,4,3,1,2,0:T(8,128)(2,1)} %convolution_convert_fusion.10), channel_id=1, source_target_pairs={{0,3},{1,2},{2,1},{3,0},{4,7},{5,6},{6,5},{7,4},{8,11},{9,10},{10,... | collective-permute-start | bytes 3932168 | tf_op jit(solution)/shard_map/ppermute | solution.py:215
  752.1 6.6 collective-permute-start.50
  778.6 4.3 pad_slice_fusion.1
  782.9 3.1 copy.320
  787.1 3.1 copy.318
  803.2 15.4 %collective-permute-start.17 = (bf16[2,2,2,2,2,16,320]{6,5,2,3,0,1,4:T(8,128)(2,1)}, bf16[2,2,2,2,2,16,320]{6,5,2,3,0,1,4:T(8,128)(2,1)}, u32[]{:S(2)}, u32[]{:S(2)}) collective-permute-start(bf16[2,2,2,2,2,16,320]{6,5,2,3,0,1,4:T(8,128)(2,1)} %convolution_convert_fusion.18), channel_id=1, source_target_pairs={{0,4},{1,5},{2,6},{3,7},{4,0},{5,1},{6,2},{7,3},{8,12},{9,13},{10,... | collective-permute-start | bytes 983048 | tf_op jit(solution)/shard_map/ppermute | solution.py:215
  824.4 4.1 collective-permute-done.17
  832.7 8.1 collective-permute-done.5
  845.3 4.9 collective-permute-done.18
  857.5 4.2 collective-permute-done.19
  862.0 5.5 collective-permute-done.15
  868.9 5.2 collective-permute-done.7
  874.2 4.6 collective-permute-done.16
  879.4 5.9 collective-permute-done.3
  886.9 4.0 collective-permute-start.22
  894.5 5.8 collective-permute-done.4
  901.6 4.9 collective-permute-done.10
  907.9 4.9 collective-permute-done.23
  913.3 5.2 collective-permute-done.24
  918.9 5.0 collective-permute-done.25
  923.9 5.5 collective-permute-done.11
  930.9 3.1 collective-permute-done.12
  937.8 18.5 %collective-permute-done.13 = bf16[16,1408]{1,0:T(8,128)(2,1)S(1)} collective-permute-done((bf16[16,1408]{1,0:T(8,128)(2,1)S(1)}, bf16[16,1408]{1,0:T(8,128)(2,1)S(1)}, u32[]{:S(2)}, u32[]{:S(2)}) %collective-permute-start.13) | collective-permute-done | bytes 45088 | tf_op jit(solution)/shard_map/ppermute | solution.py:215
  970.2 14.3 %collective-permute-done.35 = bf16[2,2,2,2,2,16,1280]{6,5,3,1,0,4,2:T(8,128)(2,1)S(1)} collective-permute-done((bf16[2,2,2,2,2,16,1280]{6,5,3,1,0,4,2:T(8,128)(2,1)S(1)}, bf16[2,2,2,2,2,16,1280]{6,5,3,1,0,4,2:T(8,128)(2,1)S(1)}, u32[]{:S(2)}, u32[]{:S(2)}) %collective-permute-start.35) | collective-permute-done | bytes 1310752 | tf_op jit(solution)/shard_map/ppermute | solution.py:215
  988.0 3.6 collective-permute-done.51
  994.3 3.6 collective-permute-start.46
  998.0 8.2 collective-permute-done.52
  1006.2 5.0 collective-permute-start.31
  1011.5 6.4 collective-permute-done.53
  1021.4 5.7 collective-permute-done.54
  1028.2 4.3 collective-permute-done.55
  1035.0 4.1 collective-permute-done.47
  1049.0 3.6 collective-permute-done.41
  1056.2 3.2 collective-permute-done.42
  1061.7 3.5 collective-permute-done.43
  (635 shorter events, 279.9 us)
Async XLA Ops:
  14.8 361.1 %all-to-all-start = ((bf16[64,1,168,960]{3,2,1,0:T(8,128)(2,1)}), bf16[64,1,168,960]{3,2,1,0:T(8,128)(2,1)}, u32[]{:S(2)}, u32[]{:S(2)}) async-start(bf16[64,1,168,960]{3,2,1,0:T(8,128)(2,1)} %stack.3), calls=%async_computation | async-start | bytes 44040192 | tf_op jit(solution)/shard_map/all_to_all | solution.py:293
  28.5 390.4 %copy-start.54 = (f32[2,64,32]{1,2,0:T(8,128)}, f32[2,64,32]{1,2,0:T(8,128)S(1)}, u32[]{:S(2)}) copy-start(f32[2,64,32]{1,2,0:T(8,128)S(1)} %get-tuple-element.166) | copy-start | bytes 49156
  443.6 231.9 %copy-start.78 = (f32[960]{0:T(1024)}, f32[960]{0:T(1024)S(1)}, u32[]{:S(2)}) copy-start(f32[960]{0:T(1024)S(1)} %mul.578) | copy-start | bytes 11524
  581.4 7.3 collective-permute-start
  677.8 5.0 collective-permute-start.1
  716.5 43.8 %copy-start.65 = (bf16[2,2,2,2,2,16,128]{6,5,4,3,2,1,0:T(8,128)(2,1)S(1)}, bf16[2,2,2,2,2,16,128]{6,5,4,3,2,1,0:T(8,128)(2,1)}, u32[]{:S(2)}) copy-start(bf16[2,2,2,2,2,16,128]{6,5,4,3,2,1,0:T(8,128)(2,1)} %get-tuple-element.131) | copy-start | bytes 393220
  718.5 43.3 %copy-start.62 = (bf16[512,128]{1,0:T(8,128)(2,1)S(1)}, bf16[512,128]{1,0:T(8,128)(2,1)}, u32[]{:S(2)}) copy-start(bf16[512,128]{1,0:T(8,128)(2,1)} %get-tuple-element.133) | copy-start | bytes 393220
  720.5 238.1 %collective-permute-start.44 = (bf16[2,2,2,2,2,40,512]{6,5,4,3,1,2,0:T(8,128)(2,1)}, bf16[2,2,2,2,2,40,512]{6,5,4,3,1,2,0:T(8,128)(2,1)}, u32[]{:S(2)}, u32[]{:S(2)}) collective-permute-start(bf16[2,2,2,2,2,40,512]{6,5,4,3,1,2,0:T(8,128)(2,1)} %convolution_convert_fusion.10), channel_id=1, source_target_pairs={{0,3},{1,2},{2,1},{3,0},{4,7},{5,6},{6,5},{7,4},{8,11},{9,10},{10,... | collective-permute-start | bytes 3932168 | tf_op jit(solution)/shard_map/ppermute | solution.py:215
  752.1 182.3 %collective-permute-start.50 = (bf16[2,2,2,2,2,40,448]{6,5,4,0,2,3,1:T(8,128)(2,1)}, bf16[2,2,2,2,2,40,448]{6,5,4,0,2,3,1:T(8,128)(2,1)}, u32[]{:S(2)}, u32[]{:S(2)}) collective-permute-start(bf16[2,2,2,2,2,40,448]{6,5,4,0,2,3,1:T(8,128)(2,1)} %convolution_convert_fusion.8), channel_id=1, source_target_pairs={{0,1},{1,0},{2,3},{3,2},{4,5},{5,4},{6,7},{7,6},{8,9},{9,8},{10,11... | collective-permute-start | bytes 3440648 | tf_op jit(solution)/shard_map/ppermute | solution.py:215
  787.1 65.2 %collective-permute-start.2 = (bf16[2,2,2,2,2,16,512]{6,5,4,2,0,3,1:T(8,128)(2,1)}, bf16[2,2,2,2,2,16,512]{6,5,4,2,0,3,1:T(8,128)(2,1)}, u32[]{:S(2)}, u32[]{:S(2)}) collective-permute-start(bf16[2,2,2,2,2,16,512]{6,5,4,2,0,3,1:T(8,128)(2,1)} %fusion.34), channel_id=1, source_target_pairs={{0,48},{1,49},{2,50},{3,51},{4,52},{5,53},{6,54},{7,55},{8,56},{9,... | collective-permute-start | bytes 1572872 | tf_op jit(solution)/shard_map/ppermute | solution.py:215
  803.2 25.3 %collective-permute-start.17 = (bf16[2,2,2,2,2,16,320]{6,5,2,3,0,1,4:T(8,128)(2,1)}, bf16[2,2,2,2,2,16,320]{6,5,2,3,0,1,4:T(8,128)(2,1)}, u32[]{:S(2)}, u32[]{:S(2)}) collective-permute-start(bf16[2,2,2,2,2,16,320]{6,5,2,3,0,1,4:T(8,128)(2,1)} %convolution_convert_fusion.18), channel_id=1, source_target_pairs={{0,4},{1,5},{2,6},{3,7},{4,0},{5,1},{6,2},{7,3},{8,12},{9,13},{10,... | collective-permute-start | bytes 983048 | tf_op jit(solution)/shard_map/ppermute | solution.py:215
  819.7 11.5 %collective-permute-start.14 = (bf16[2,2,2,2,2,16,384]{6,5,1,3,0,4,2:T(8,128)(2,1)}, bf16[2,2,2,2,2,16,384]{6,5,1,3,0,4,2:T(8,128)(2,1)}, u32[]{:S(2)}, u32[]{:S(2)}) collective-permute-start(bf16[2,2,2,2,2,16,384]{6,5,1,3,0,4,2:T(8,128)(2,1)} %convolution_convert_fusion.20), channel_id=1, source_target_pairs={{0,16},{1,17},{2,18},{3,19},{4,20},{5,21},{6,22},{7,23},{8,24},{9,... | collective-permute-start | bytes 1179656 | tf_op jit(solution)/shard_map/ppermute | solution.py:215
  828.5 12.3 %collective-permute-start.5 = (bf16[2,2,2,2,2,16,384]{6,5,4,2,1,3,0:T(8,128)(2,1)}, bf16[2,2,2,2,2,16,384]{6,5,4,2,1,3,0:T(8,128)(2,1)S(1)}, u32[]{:S(2)}, u32[]{:S(2)}) collective-permute-start(bf16[2,2,2,2,2,16,384]{6,5,4,2,1,3,0:T(8,128)(2,1)} %convolution_convert_fusion.22), channel_id=1, source_target_pairs={{0,12},{1,13},{2,14},{3,15},{4,8},{5,9},{6,10},{7,11},{8,4},{9,5},... | collective-permute-start | bytes 1179656 | tf_op jit(solution)/shard_map/ppermute | solution.py:215
  831.2 13.2 %collective-permute-start.20 = (bf16[2,2,2,2,2,16,448]{6,5,2,4,0,3,1:T(8,128)(2,1)}, bf16[2,2,2,2,2,16,448]{6,5,2,4,0,3,1:T(8,128)(2,1)S(1)}, u32[]{:S(2)}, u32[]{:S(2)}) collective-permute-start(bf16[2,2,2,2,2,16,448]{6,5,2,4,0,3,1:T(8,128)(2,1)} %convolution_convert_fusion.12), channel_id=1, source_target_pairs={{0,1},{1,0},{2,3},{3,2},{4,5},{5,4},{6,7},{7,6},{8,9},{9,8},{10,11... | collective-permute-start | bytes 1376264 | tf_op jit(solution)/shard_map/ppermute | solution.py:215
  840.7 15.5 %collective-permute-start.8 = (bf16[2,2,2,2,2,16,512]{6,5,4,3,1,2,0:T(8,128)(2,1)}, bf16[2,2,2,2,2,16,512]{6,5,4,3,1,2,0:T(8,128)(2,1)S(1)}, u32[]{:S(2)}, u32[]{:S(2)}) collective-permute-start(bf16[2,2,2,2,2,16,512]{6,5,4,3,1,2,0:T(8,128)(2,1)} %convolution_convert_fusion.14), channel_id=1, source_target_pairs={{0,3},{1,2},{2,1},{3,0},{4,7},{5,6},{6,5},{7,4},{8,11},{9,10},{10,... | collective-permute-start | bytes 1572872 | tf_op jit(solution)/shard_map/ppermute | solution.py:215
  844.5 5.7 collective-permute-start.18
  850.1 111.6 %collective-permute-start.29 = (bf16[2,2,2,2,2,16,1280]{6,5,4,2,1,3,0:T(8,128)(2,1)}, bf16[2,2,2,2,2,16,1280]{6,5,4,2,1,3,0:T(8,128)(2,1)}, u32[]{:S(2)}, u32[]{:S(2)}) collective-permute-start(bf16[2,2,2,2,2,16,1280]{6,5,4,2,1,3,0:T(8,128)(2,1)} %convolution_convert_fusion.4), channel_id=1, source_target_pairs={{0,12},{1,13},{2,14},{3,15},{4,8},{5,9},{6,10},{7,11},{8,4},{9,5},... | collective-permute-start | bytes 3932168 | tf_op jit(solution)/shard_map/ppermute | solution.py:215
  852.2 9.6 collective-permute-start.6
  856.2 5.6 collective-permute-start.19
  861.8 5.7 collective-permute-start.15
  861.8 6.5 collective-permute-start.21
  862.0 74.1 %copy-start.6 = (bf16[2,2,2,2,2,40,448]{6,5,4,0,2,3,1:T(8,128)(2,1)S(1)}, bf16[2,2,2,2,2,40,448]{6,5,4,0,2,3,1:T(8,128)(2,1)}, u32[]{:S(2)}) copy-start(bf16[2,2,2,2,2,40,448]{6,5,4,0,2,3,1:T(8,128)(2,1)} %convolution_convert_fusion.9) | copy-start | bytes 3440644
  867.5 17.8 %collective-permute-start.3 = (bf16[2,2,2,2,16,512]{5,4,3,2,1,0:T(8,128)(2,1)S(1)}, bf16[2,2,2,2,16,512]{5,4,3,2,1,0:T(8,128)(2,1)S(1)}, u32[]{:S(2)}, u32[]{:S(2)}) collective-permute-start(bf16[2,2,2,2,16,512]{5,4,3,2,1,0:T(8,128)(2,1)S(1)} %fusion.147), channel_id=1, source_target_pairs={{0,12},{1,13},{2,14},{3,15},{4,8},{5,9},{6,10},{7,11},{8,4},{9,5},... | collective-permute-start | bytes 786440 | tf_op jit(solution)/shard_map/ppermute | solution.py:215
  868.3 5.8 collective-permute-start.7
  874.1 4.6 collective-permute-start.16
  878.7 8.1 collective-permute-start.9
  885.2 79.9 %collective-permute-start.26 = (bf16[2,2,2,2,2,16,1280]{6,5,4,2,0,3,1:T(8,128)(2,1)}, bf16[2,2,2,2,2,16,1280]{6,5,4,2,0,3,1:T(8,128)(2,1)}, u32[]{:S(2)}, u32[]{:S(2)}) collective-permute-start(bf16[2,2,2,2,2,16,1280]{6,5,4,2,0,3,1:T(8,128)(2,1)} %convolution_convert_fusion.6), channel_id=1, source_target_pairs={{0,48},{1,49},{2,50},{3,51},{4,52},{5,53},{6,54},{7,55},{8,56},{9,... | collective-permute-start | bytes 3932168 | tf_op jit(solution)/shard_map/ppermute | solution.py:215
  886.9 7.0 collective-permute-start.22
  893.8 6.5 collective-permute-start.4
  894.5 61.9 %copy-start.35 = (bf16[2,2,2,2,2,16,1280]{6,5,3,1,0,4,2:T(8,128)(2,1)S(1)}, bf16[2,2,2,2,2,16,1280]{6,5,3,1,0,4,2:T(8,128)(2,1)}, u32[]{:S(2)}) copy-start(bf16[2,2,2,2,2,16,1280]{6,5,3,1,0,4,2:T(8,128)(2,1)} %convolution_convert_fusion.2) | copy-start | bytes 3932164
  900.3 6.2 collective-permute-start.10
  906.5 6.4 collective-permute-start.23
  907.9 52.5 %copy-start.2 = (bf16[2,2,2,2,2,40,512]{6,5,4,3,2,1,0:T(8,128)(2,1)S(1)}, bf16[2,2,2,2,2,40,512]{6,5,4,3,2,1,0:T(8,128)(2,1)}, u32[]{:S(2)}) copy-start(bf16[2,2,2,2,2,40,512]{6,5,4,3,2,1,0:T(8,128)(2,1)} %convolution_convert_fusion.11) | copy-start | bytes 3932164
  912.9 5.6 collective-permute-start.24
  918.6 5.2 collective-permute-start.25
  923.8 5.5 collective-permute-start.11
  929.4 4.6 collective-permute-start.12
  934.0 33.1 %collective-permute-start.38 = (bf16[2,2,2,2,2,16,1280]{6,5,3,2,0,1,4:T(8,128)(2,1)S(1)}, bf16[2,2,2,2,2,16,1280]{6,5,3,2,0,1,4:T(8,128)(2,1)S(1)}, u32[]{:S(2)}, u32[]{:S(2)}) collective-permute-start(bf16[2,2,2,2,2,16,1280]{6,5,3,2,0,1,4:T(8,128)(2,1)S(1)} %copy-done.36), channel_id=1, source_target_pairs={{0,4},{1,5},{2,6},{3,7},{4,0},{5,1},{6,2},{7,3},{8,12},{9,13},{10,... | collective-permute-start | bytes 3932168 | tf_op jit(solution)/shard_map/ppermute | solution.py:215
  934.4 22.0 %collective-permute-start.13 = (bf16[16,1408]{1,0:T(8,128)(2,1)S(1)}, bf16[16,1408]{1,0:T(8,128)(2,1)S(1)}, u32[]{:S(2)}, u32[]{:S(2)}) collective-permute-start(bf16[16,1408]{1,0:T(8,128)(2,1)S(1)} %fusion.253), channel_id=1, source_target_pairs={{0,4},{1,5},{2,6},{3,7},{4,0},{5,1},{6,2},{7,3},{8,12},{9,13},{10,... | collective-permute-start | bytes 135176 | tf_op jit(solution)/shard_map/ppermute | solution.py:215
  956.4 28.1 %collective-permute-start.35 = (bf16[2,2,2,2,2,16,1280]{6,5,3,1,0,4,2:T(8,128)(2,1)S(1)}, bf16[2,2,2,2,2,16,1280]{6,5,3,1,0,4,2:T(8,128)(2,1)S(1)}, u32[]{:S(2)}, u32[]{:S(2)}) collective-permute-start(bf16[2,2,2,2,2,16,1280]{6,5,3,1,0,4,2:T(8,128)(2,1)S(1)} %copy-done.35), channel_id=1, source_target_pairs={{0,16},{1,17},{2,18},{3,19},{4,20},{5,21},{6,22},{7,23},{8,24},{9,... | collective-permute-start | bytes 3932168 | tf_op jit(solution)/shard_map/ppermute | solution.py:215
  958.7 32.8 %collective-permute-start.51 = (bf16[2,2,2,2,40,448]{5,4,3,0,1,2:T(8,128)(2,1)S(1)}, bf16[2,2,2,2,40,448]{5,4,3,0,1,2:T(8,128)(2,1)S(1)}, u32[]{:S(2)}, u32[]{:S(2)}) collective-permute-start(bf16[2,2,2,2,40,448]{5,4,3,0,1,2:T(8,128)(2,1)S(1)} %get-tuple-element.61), channel_id=1, source_target_pairs={{0,16},{1,17},{2,18},{3,19},{4,20},{5,21},{6,22},{7,23},{8,24},{9,... | collective-permute-start | bytes 1720328 | tf_op jit(solution)/shard_map/ppermute | solution.py:215
  961.7 32.4 %collective-permute-start.45 = (bf16[2,2,2,2,40,512]{5,4,3,2,1,0:T(8,128)(2,1)S(1)}, bf16[2,2,2,2,40,512]{5,4,3,2,1,0:T(8,128)(2,1)S(1)}, u32[]{:S(2)}, u32[]{:S(2)}) collective-permute-start(bf16[2,2,2,2,40,512]{5,4,3,2,1,0:T(8,128)(2,1)S(1)} %fusion.68), channel_id=1, source_target_pairs={{0,48},{1,49},{2,50},{3,51},{4,52},{5,53},{6,54},{7,55},{8,56},{9,... | collective-permute-start | bytes 1966088 | tf_op jit(solution)/shard_map/ppermute | solution.py:215
  965.1 29.2 %collective-permute-start.30 = (bf16[2,2,2,2,16,1280]{5,4,3,2,1,0:T(8,128)(2,1)S(1)}, bf16[2,2,2,2,16,1280]{5,4,3,2,1,0:T(8,128)(2,1)S(1)}, u32[]{:S(2)}, u32[]{:S(2)}) collective-permute-start(bf16[2,2,2,2,16,1280]{5,4,3,2,1,0:T(8,128)(2,1)S(1)} %get-tuple-element.63), channel_id=1, source_target_pairs={{0,3},{1,2},{2,1},{3,0},{4,7},{5,6},{6,5},{7,4},{8,11},{9,10},{10,... | collective-permute-start | bytes 1966088 | tf_op jit(solution)/shard_map/ppermute | solution.py:215
  967.1 44.2 %collective-permute-start.27 = (bf16[2,2,2,2,16,1280]{5,4,3,2,1,0:T(8,128)(2,1)S(1)}, bf16[2,2,2,2,16,1280]{5,4,3,2,1,0:T(8,128)(2,1)S(1)}, u32[]{:S(2)}, u32[]{:S(2)}) collective-permute-start(bf16[2,2,2,2,16,1280]{5,4,3,2,1,0:T(8,128)(2,1)S(1)} %fusion.67), channel_id=1, source_target_pairs={{0,12},{1,13},{2,14},{3,15},{4,8},{5,9},{6,10},{7,11},{8,4},{9,5},... | collective-permute-start | bytes 1966088 | tf_op jit(solution)/shard_map/ppermute | solution.py:215
  984.5 34.4 %collective-permute-start.39 = (bf16[2,2,2,2,16,1280]{5,4,3,2,0,1:T(8,128)(2,1)S(1)}, bf16[2,2,2,2,16,1280]{5,4,3,2,0,1:T(8,128)(2,1)S(1)}, u32[]{:S(2)}, u32[]{:S(2)}) collective-permute-start(bf16[2,2,2,2,16,1280]{5,4,3,2,0,1:T(8,128)(2,1)S(1)} %get-tuple-element.65), channel_id=1, source_target_pairs={{0,1},{1,0},{2,3},{3,2},{4,5},{5,4},{6,7},{7,6},{8,9},{9,8},{10,11... | collective-permute-start | bytes 1966088 | tf_op jit(solution)/shard_map/ppermute | solution.py:215
  991.5 35.6 %collective-permute-start.36 = (bf16[2,2,2,2,16,1280]{5,4,2,1,0,3:T(8,128)(2,1)S(1)}, bf16[2,2,2,2,16,1280]{5,4,2,1,0,3:T(8,128)(2,1)S(1)}, u32[]{:S(2)}, u32[]{:S(2)}) collective-permute-start(bf16[2,2,2,2,16,1280]{5,4,2,1,0,3:T(8,128)(2,1)S(1)} %get-tuple-element.67), channel_id=1, source_target_pairs={{0,4},{1,5},{2,6},{3,7},{4,0},{5,1},{6,2},{7,3},{8,12},{9,13},{10,... | collective-permute-start | bytes 1966088 | tf_op jit(solution)/shard_map/ppermute | solution.py:215
  994.1 12.1 %collective-permute-start.52 = (bf16[2,2,2,40,448]{4,3,2,0,1:T(8,128)(2,1)S(1)}, bf16[2,2,2,40,448]{4,3,2,0,1:T(8,128)(2,1)S(1)}, u32[]{:S(2)}, u32[]{:S(2)}) collective-permute-start(bf16[2,2,2,40,448]{4,3,2,0,1:T(8,128)(2,1)S(1)} %fusion.122), channel_id=1, source_target_pairs={{0,4},{1,5},{2,6},{3,7},{4,0},{5,1},{6,2},{7,3},{8,12},{9,13},{10,... | collective-permute-start | bytes 860168 | tf_op jit(solution)/shard_map/ppermute | solution.py:215
  994.3 38.2 %collective-permute-start.46 = (bf16[2,2,2,40,512]{4,3,2,1,0:T(8,128)(2,1)S(1)}, bf16[2,2,2,40,512]{4,3,2,1,0:T(8,128)(2,1)S(1)}, u32[]{:S(2)}, u32[]{:S(2)}) collective-permute-start(bf16[2,2,2,40,512]{4,3,2,1,0:T(8,128)(2,1)S(1)} %fusion.126), channel_id=1, source_target_pairs={{0,12},{1,13},{2,14},{3,15},{4,8},{5,9},{6,10},{7,11},{8,4},{9,5},... | collective-permute-start | bytes 983048 | tf_op jit(solution)/shard_map/ppermute | solution.py:215
  1006.2 27.1 %collective-permute-start.31 = (bf16[2,2,2,16,1280]{4,3,2,1,0:T(8,128)(2,1)S(1)}, bf16[2,2,2,16,1280]{4,3,2,1,0:T(8,128)(2,1)S(1)}, u32[]{:S(2)}, u32[]{:S(2)}) collective-permute-start(bf16[2,2,2,16,1280]{4,3,2,1,0:T(8,128)(2,1)S(1)} %fusion.125), channel_id=1, source_target_pairs={{0,48},{1,49},{2,50},{3,51},{4,52},{5,53},{6,54},{7,55},{8,56},{9,... | collective-permute-start | bytes 983048 | tf_op jit(solution)/shard_map/ppermute | solution.py:215
  1011.3 6.6 collective-permute-start.53
  1018.0 15.4 %collective-permute-start.28 = (bf16[2,2,2,16,1280]{4,3,2,1,0:T(8,128)(2,1)S(1)}, bf16[2,2,2,16,1280]{4,3,2,1,0:T(8,128)(2,1)S(1)}, u32[]{:S(2)}, u32[]{:S(2)}) collective-permute-start(bf16[2,2,2,16,1280]{4,3,2,1,0:T(8,128)(2,1)S(1)} %fusion.123), channel_id=1, source_target_pairs={{0,3},{1,2},{2,1},{3,0},{4,7},{5,6},{6,5},{7,4},{8,11},{9,10},{10,... | collective-permute-start | bytes 983048 | tf_op jit(solution)/shard_map/ppermute | solution.py:215
  1018.9 8.2 collective-permute-start.54
  1027.1 7.7 collective-permute-start.40
  1027.2 5.3 collective-permute-start.55
  1032.4 8.9 collective-permute-start.37
  1032.6 6.4 collective-permute-start.47
  1033.6 15.0 %collective-permute-start.32 = (bf16[2,2,16,2560]{3,2,1,0:T(8,128)(2,1)S(1)}, bf16[2,2,16,2560]{3,2,1,0:T(8,128)(2,1)S(1)}, u32[]{:S(2)}, u32[]{:S(2)}) collective-permute-start(bf16[2,2,16,2560]{3,2,1,0:T(8,128)(2,1)S(1)} %fusion.130), channel_id=1, source_target_pairs={{0,16},{1,17},{2,18},{3,19},{4,20},{5,21},{6,22},{7,23},{8,24},{9,... | collective-permute-start | bytes 983048 | tf_op jit(solution)/shard_map/ppermute | solution.py:215
  1039.1 4.7 collective-permute-start.48
  1043.8 4.1 collective-permute-start.49
  1044.3 8.4 collective-permute-start.41
  1048.6 5.4 collective-permute-start.33
  1052.8 6.6 collective-permute-start.42
  1054.1 7.5 collective-permute-start.34
  1059.4 5.7 collective-permute-start.43
  (131 other events, 1232.8 us)
